TPU v7x, 128 devices: a whole 4x4x4 slice. The times are simulated.
128 devices in a mesh: arc: 16 (over x, z), vec: 8 (over y, core).
Axes of the slice: x: 4, y: 4, z: 4, core: 2. Of those that a mesh axis runs over, the one named last changes fastest.
Arguments:
- right_side: float32 [640, 128, 128], P(('arc', 'vec')), may hold values from -6 to 6
- prior_diag: float32 [640, 128], P(('arc', 'vec')), may hold values from 0.5 to 4
- inv_factor: bfloat16 [2048, 256, 256], P(('arc', 'vec'))
- coupling_panel: bfloat16 [2048, 256, 1024], P(('arc', 'vec')), may hold values from -0.09375 to 0.09375
- coupling_owner: int32 [2048, 8], replicated, may hold values from 0 to 127, all different within a row; in each aligned block of 16 rows (0 to 15, 16 to 31, ...) at most 2 rows name the same one
- coupling_block: int32 [2048, 8], replicated, may hold values from 0 to 4
Outputs:
- solution_field: float32 [640, 128, 128], P(('arc', 'vec'))
- residual: float32 [640, 128, 128], P(('arc', 'vec'))
Inputs may be any that keep to these rules, and one draw needn't show every extreme that they name: `coupling_owner`: the 8 holders named for one arc are different. Among the 16 arcs of one device (aligned blocks of rows) no holder is named more than 2 times; some holder is named exactly 2 times.
All inputs are finite; a program needn't handle non-finite values.
Results may differ from a plain program's by a relative error of at most 0.006.
The roundings to bfloat16 on the way count: a program that leaves them out, or rounds other values in their place, can miss the bound.
Values may be sent and summed in bfloat16 or wider, within the bound.
A program may use at most 128 MiB of HBM per device.

v0:
```python
import jax
import jax.numpy as jnp
from jax import lax
from jax.sharding import PartitionSpec as P

ITERS = 2


def inner_gram(left, right):
    return jnp.einsum("grc,grd->cd", left, right, precision=lax.Precision.HIGHEST)


def combine_cols(field, weights):
    return jnp.einsum("grc,cd->grd", field, weights, precision=lax.Precision.HIGHEST)


def trade_out(buffer):
    return lax.all_to_all(buffer, ("arc", "vec"), split_axis=0, concat_axis=0, tiled=True)


def trade_back(buffer):
    return lax.all_to_all(buffer, ("arc", "vec"), split_axis=0, concat_axis=0, tiled=True)


def per_device(right_side, prior_diag, inv_factor, coupling_panel, coupling_owner, coupling_block):
    device_count = lax.axis_size(("arc", "vec"))
    my_index = lax.axis_index(("arc", "vec"))
    arcs_here = coupling_panel.shape[0]
    links = coupling_owner.shape[1]
    blocks_here = right_side.shape[0]
    block_rows = right_side.shape[1]
    rhs_count = right_side.shape[2]
    entries = arcs_here * links
    slot_count = (entries + device_count - 1) // device_count + 1
    owner_all = coupling_owner.reshape(device_count, entries)
    block_all = coupling_block.reshape(device_count, entries)
    position = jnp.arange(entries, dtype=jnp.int32)
    earlier = (owner_all[:, :, None] == owner_all[:, None, :]) & (
        position[None, None, :] < position[None, :, None]
    )
    rank_all = jnp.sum(earlier.astype(jnp.int32), axis=2)
    owner_mine = lax.dynamic_index_in_dim(owner_all, my_index, 0, keepdims=False)
    rank_mine = lax.dynamic_index_in_dim(rank_all, my_index, 0, keepdims=False)
    slot_mine = owner_mine * slot_count + rank_mine
    slot_ids = jnp.arange(slot_count, dtype=jnp.int32)
    matches = (owner_all[:, None, :] == my_index) & (
        rank_all[:, None, :] == slot_ids[None, :, None]
    )
    filled = jnp.any(matches, axis=2).reshape(-1)
    source_block = jnp.sum(jnp.where(matches, block_all[:, None, :], 0), axis=2).reshape(-1)
    block_ids = jnp.arange(blocks_here, dtype=jnp.int32)
    selector = ((source_block[:, None] == block_ids[None, :]) & filled[:, None]).astype(
        jnp.bfloat16
    )
    solution_field = jnp.zeros_like(right_side)
    residual = right_side
    direction = right_side
    res_gram = lax.psum(inner_gram(residual, residual), ("arc", "vec"))
    for sweep_index in range(ITERS):
        local_rounded = direction.astype(jnp.bfloat16)
        outgoing = jnp.where(
            filled[:, None, None], local_rounded[source_block], jnp.zeros((), jnp.bfloat16)
        )
        arrived = trade_out(outgoing)
        fetched = arrived[slot_mine].reshape(arcs_here, links * block_rows, rhs_count)
        coupled = jnp.einsum(
            "apk,akc->apc", coupling_panel, fetched, preferred_element_type=jnp.float32
        ).astype(jnp.bfloat16)
        whitened = jnp.einsum(
            "apq,aqc->apc", inv_factor, coupled, preferred_element_type=jnp.float32
        ).astype(jnp.bfloat16)
        smoothed = jnp.einsum(
            "aqp,aqc->apc", inv_factor, whitened, preferred_element_type=jnp.float32
        ).astype(jnp.bfloat16)
        projected = jnp.einsum(
            "apk,apc->akc", coupling_panel, smoothed, preferred_element_type=jnp.float32
        ).astype(jnp.bfloat16)
        projected = projected.reshape(entries, block_rows, rhs_count)
        returning = (
            jnp.zeros((device_count * slot_count, block_rows, rhs_count), jnp.bfloat16)
            .at[slot_mine]
            .set(projected)
        )
        came_back = trade_back(returning)
        summed = jnp.einsum("sb,src->brc", selector, came_back, preferred_element_type=jnp.float32)
        image_vec = prior_diag[:, :, None] * direction + summed
        curv_gram = lax.psum(inner_gram(direction, image_vec), ("arc", "vec"))
        factor_low = jnp.linalg.cholesky(curv_gram)
        step_mat = jax.scipy.linalg.cho_solve((factor_low, True), res_gram)
        solution_field = solution_field + combine_cols(direction, step_mat)
        residual = residual - combine_cols(image_vec, step_mat)
        if sweep_index + 1 < ITERS:
            new_gram = lax.psum(inner_gram(residual, residual), ("arc", "vec"))
            beta_mat = jax.scipy.linalg.cho_solve((jnp.linalg.cholesky(res_gram), True), new_gram)
            direction = residual + combine_cols(direction, beta_mat)
            res_gram = new_gram
    return (solution_field, residual)


def solution(mesh):
    in_specs = (
        P(("arc", "vec"), None, None),
        P(("arc", "vec"), None),
        P(("arc", "vec"), None, None),
        P(("arc", "vec"), None, None),
        P(),
        P(),
    )
    out_specs = (P(("arc", "vec"), None, None), P(("arc", "vec"), None, None))
    return jax.shard_map(
        per_device, mesh=mesh, in_specs=in_specs, out_specs=out_specs, check_vma=False
    )
```

profile of v0, /device:TPU:1, one launch (start us, length us, event | category | flops | bytes accessed | tf_op | source)
XLA Modules:
  0.0 1105.9 jit_solution(6747091864298645977)
XLA Ops:
  17.7 8.3 gather_fusion
  26.0 7.2 broadcast_select_fusion.1
  33.3 12.3 %all-to-all-start = ((bf16[256,128,128]{2,1,0:T(8,128)(2,1)}), bf16[256,128,128]{2,1,0:T(8,128)(2,1)}, u32[]{:S(2)}, u32[]{:S(2)}) async-start(bf16[256,128,128]{2,1,0:T(8,128)(2,1)} %broadcast_select_fusion.1), calls=%async_computation | async-start | bytes 16777216 | tf_op jit(solution)/shard_map/all_to_all | solution.py:18
  45.7 106.4 %all-to-all-done = bf16[256,128,128]{2,1,0:T(8,128)(2,1)} async-done(((bf16[256,128,128]{2,1,0:T(8,128)(2,1)}), bf16[256,128,128]{2,1,0:T(8,128)(2,1)}, u32[]{:S(2)}, u32[]{:S(2)}) %all-to-all-start) | async-done | bytes 8388640 | tf_op jit(solution)/shard_map/all_to_all | solution.py:18
  152.0 6.4 gather_fusion.1
  158.5 8.2 convolution_convert_fusion.4
  166.7 6.9 convert_bitcast_fusion.1
  173.6 6.4 copy.140
  180.0 5.3 broadcast.116.clone
  185.3 19.4 %scatter_fusion = bf16[256,128,128]{2,1,0:T(8,128)(2,1)} fusion(bf16[256,128,128]{2,1,0:T(8,128)(2,1)} %broadcast.116.clone, s32[128]{0:T(128)S(1)} %fusion.34, bf16[128,128,128]{2,1,0:T(8,128)(2,1)} %bitcast.106), kind=kCustom, calls=%fused_computation.4 | custom fusion | bytes 12583424 | tf_op jit(solution)/shard_map/scatter | solution.py:82
  204.7 6.8 all-to-all-start.1
  213.2 104.7 %all-to-all-done.1 = bf16[256,128,128]{2,1,0:T(8,128)(2,1)} async-done(((bf16[256,128,128]{2,1,0:T(8,128)(2,1)}), bf16[256,128,128]{2,1,0:T(8,128)(2,1)}, u32[]{:S(2)}, u32[]{:S(2)}) %all-to-all-start.1) | async-done | bytes 8388640 | tf_op jit(solution)/shard_map/all_to_all | solution.py:22
  317.9 7.8 fusion.2
  327.5 139.7 %all-reduce.9.cloned.1.call-done = (f32[128,128]{0,1:T(8,128)}, f32[128,128]{0,1:T(8,128)}) async-done(((f32[128,128]{0,1:T(8,128)}, f32[128,128]{0,1:T(8,128)}), (f32[128,128]{0,1:T(8,128)}, f32[128,128]{0,1:T(8,128)})) %all-reduce.9.cloned.1.call-update) | async-done | bytes 131088 | tf_op jit(solution)/shard_map/psum | solution.py:58
  470.0 11.7 %cholesky.70 = f32[128,128]{1,0:T(8,128)S(1)} custom-call(f32[128,128]{1,0:T(8,128)S(1)} %get-tuple-element.18), custom_call_target="Cholesky" | custom-call | tf_op jit(solution)/shard_map/jit(cholesky)/cholesky | solution.py:94
  482.4 11.7 %cholesky.59 = f32[128,128]{1,0:T(8,128)S(1)} custom-call(f32[128,128]{1,0:T(8,128)S(1)} %get-tuple-element.19), custom_call_target="Cholesky" | custom-call | tf_op jit(solution)/shard_map/jit(cholesky)/cholesky | solution.py:88
  495.5 9.8 custom-call.9
  508.4 10.2 all-reduce.7.cloned.1.call-start
  520.1 9.8 custom-call.10
  530.0 114.2 %all-reduce.5.cloned.1.call-done = f32[128,128]{1,0:T(8,128)} async-done(((f32[128,128]{1,0:T(8,128)}), f32[128,128]{1,0:T(8,128)}) %all-reduce.5.cloned.1.call-update) | async-done | bytes 65552 | tf_op jit(solution)/shard_map/psum | solution.py:93
  646.0 8.3 gather_fusion.2
  654.4 7.2 broadcast_select_fusion
  661.6 103.7 %all_to_all.20 = bf16[256,128,128]{2,1,0:T(8,128)(2,1)} all-to-all(bf16[256,128,128]{2,1,0:T(8,128)(2,1)} %broadcast_select_fusion), channel_id=1, replica_groups=mesh['arc'=16,'vec'=8] {'arc','vec'}, dimensions={0} | all-to-all | bytes 16777216 | tf_op jit(solution)/shard_map/all_to_all | solution.py:18
  765.3 6.4 gather_fusion.3
  771.8 9.2 convolution_convert_fusion.1
  781.0 7.2 convert_bitcast_fusion
  788.2 6.4 copy.153
  799.9 19.4 %scatter_fusion.1 = bf16[256,128,128]{2,1,0:T(8,128)(2,1)} fusion(bf16[256,128,128]{2,1,0:T(8,128)(2,1)} %broadcast.116, s32[128]{0:T(128)S(1)} %fusion.34, bf16[128,128,128]{2,1,0:T(8,128)(2,1)} %bitcast.105), kind=kCustom, calls=%fused_computation.5 | custom fusion | bytes 12583424 | tf_op jit(solution)/shard_map/scatter | solution.py:82
  819.3 106.0 %all_to_all.21 = bf16[256,128,128]{2,1,0:T(8,128)(2,1)S(1)} all-to-all(bf16[256,128,128]{2,1,0:T(8,128)(2,1)} %scatter_fusion.1), channel_id=1, replica_groups=mesh['arc'=16,'vec'=8] {'arc','vec'}, dimensions={0} | all-to-all | bytes 16777216 | tf_op jit(solution)/shard_map/all_to_all | solution.py:22
  933.2 136.1 %all-reduce.7.cloned.1.call-done = f32[128,128]{0,1:T(8,128)} async-done(((f32[128,128]{0,1:T(8,128)}), f32[128,128]{0,1:T(8,128)}) %all-reduce.7.cloned.1.call-update) | async-done | bytes 65552 | tf_op jit(solution)/shard_map/psum | solution.py:87
  1071.1 11.7 %cholesky.81 = f32[128,128]{1,0:T(8,128)S(1)} custom-call(f32[128,128]{1,0:T(8,128)S(1)} %fusion.17), custom_call_target="Cholesky" | custom-call | tf_op jit(solution)/shard_map/jit(cholesky)/cholesky | solution.py:88
  1084.2 9.8 custom-call.11
  (68 shorter events, 46.7 us)
Async XLA Ops:
  7.2 151.3 %copy-start = (bf16[16,256,256]{2,1,0:T(8,128)(2,1)S(1)}, bf16[16,256,256]{2,1,0:T(8,128)(2,1)}, u32[]{:S(2)}) copy-start(bf16[16,256,256]{2,1,0:T(8,128)(2,1)} %param.11) | copy-start | bytes 6291460
  33.3 118.8 %all-to-all-start = ((bf16[256,128,128]{2,1,0:T(8,128)(2,1)}), bf16[256,128,128]{2,1,0:T(8,128)(2,1)}, u32[]{:S(2)}, u32[]{:S(2)}) async-start(bf16[256,128,128]{2,1,0:T(8,128)(2,1)} %broadcast_select_fusion.1), calls=%async_computation | async-start | bytes 16777216 | tf_op jit(solution)/shard_map/all_to_all | solution.py:18
  204.7 7.2 copy-start.1
  204.7 113.2 %all-to-all-start.1 = ((bf16[256,128,128]{2,1,0:T(8,128)(2,1)}), bf16[256,128,128]{2,1,0:T(8,128)(2,1)}, u32[]{:S(2)}, u32[]{:S(2)}) async-start(bf16[256,128,128]{2,1,0:T(8,128)(2,1)} %scatter_fusion), calls=%async_computation.1 | async-start | bytes 16777216 | tf_op jit(solution)/shard_map/all_to_all | solution.py:22
  211.4 114.3 %copy-start.5 = (f32[5,128]{1,0:T(8,128)S(1)}, f32[5,128]{1,0:T(8,128)}, u32[]{:S(2)}) copy-start(f32[5,128]{1,0:T(8,128)} %param.10) | copy-start | bytes 7684
  211.4 255.8 %all-reduce.9.cloned.1.call-start = ((), (), s32[]{:S(2)}) async-start(), calls=%async_computation.6 | async-start | bytes 262144 | tf_op jit(solution)/shard_map/psum | solution.py:58
  327.2 317.0 %all-reduce.5.cloned.1.call-start = ((), (), s32[]{:S(2)}) async-start(), calls=%async_computation.4 | async-start | bytes 131072 | tf_op jit(solution)/shard_map/psum | solution.py:93
  481.7 13.1 %copy-start.4 = (f32[128,128]{1,0:T(8,128)}, f32[128,128]{1,0:T(8,128)S(1)}, u32[]{:S(2)}) copy-start(f32[128,128]{1,0:T(8,128)S(1)} %cholesky.70) | copy-start | bytes 196612
  508.4 560.9 %all-reduce.7.cloned.1.call-start = ((), (), s32[]{:S(2)}) async-start(), calls=%async_computation.5 | async-start | bytes 131072 | tf_op jit(solution)/shard_map/psum | solution.py:87
  925.3 168.7 %copy-start.3 = (f32[128,128]{1,0:T(8,128)S(1)}, f32[128,128]{1,0:T(8,128)}, u32[]{:S(2)}) copy-start(f32[128,128]{1,0:T(8,128)} %all-reduce.5.cloned.1.call-done) | copy-start | bytes 196612
  929.7 0.8 copy-start.2
Sparse Core Ops, SparseCore 0:
  327.3 139.8 all-reduce.8
  508.6 135.5 all-reduce.4
  932.1 137.1 all-reduce.6
where the time goes:
time: 1110 us
  waiting for transfers between devices  601 us (54%)
  blocking collectives  210 us (19%)
  local copies, waits for them, and re-layouts  100 us (9%)
  other arithmetic  92 us (8%)
  matrix products  58.4 us (5%)
  starting transfers between devices  29.9 us (3%)
  between operations  14.3 us (1%)
    psum x1, waiting for transfers between devices, per_device(): res_gram = lax.psum(inner_gram(residual, residual), ('arc', 'vec'))  140 us
    psum x1, waiting for transfers between devices, per_device(): curv_gram = lax.psum(inner_gram(direction, image_vec), ('arc', 'vec'))  136 us
    psum x1, waiting for transfers between devices, per_device(): new_gram = lax.psum(inner_gram(residual, residual), ('arc', 'vec'))  114 us
    all_to_all x1, waiting for transfers between devices, trade_out(): lax.all_to_all(buffer, ('arc', 'vec'), split_axis=0, concat_axis=0, tiled...  106 us
    all_to_all x1, blocking collectives, trade_back(): lax.all_to_all(buffer, ('arc', 'vec'), split_axis=0, concat_axis=0, tiled...  106 us
    all_to_all x1, waiting for transfers between devices, trade_back(): lax.all_to_all(buffer, ('arc', 'vec'), split_axis=0, concat_axis=0, tiled...  105 us
    all_to_all x1, blocking collectives, trade_out(): lax.all_to_all(buffer, ('arc', 'vec'), split_axis=0, concat_axis=0, tiled...  104 us
    scatter x2, local copies, waits for them, and re-layouts, per_device(): returning = jnp.zeros((device_count * slot_count, block_rows, rhs_count),...  38.7 us
  transfers between devices with their start and end apart: 5, of which 5 were waited for; matrix products, arithmetic and copies ran while one was open for 1% of the time, Pallas kernels for 0%

commit v1 on v0

--- a/solution.py
+++ b/solution.py
@@ -55,7 +55,8 @@
     solution_field = jnp.zeros_like(right_side)
     residual = right_side
     direction = right_side
-    res_gram = lax.psum(inner_gram(residual, residual), ("arc", "vec"))
+    half = lax.psum(inner_gram(residual, residual), "vec")
+    res_gram = lax.psum(half, "arc")
     for sweep_index in range(ITERS):
         local_rounded = direction.astype(jnp.bfloat16)
         outgoing = jnp.where(

time: 1110 us -> 1200 us (1.081)
  waiting for transfers between devices: 601 us -> 694 us
    psum x1 -> x2, waiting for transfers between devices: 136 us -> 273 us  [per_device(): curv_gram = lax.psum(inner_gram(direction, image_vec), ('arc', 'vec'))]
    all_to_all x1, waiting for transfers between devices: 105 us -> 0.01 us  [trade_back(): lax.all_to_all(buffer, ('arc', 'vec'), split_axis=0, concat_axis=0, tiled...]
    psum x1 -> x2, waiting for transfers between devices: 140 us -> 191 us  [the longest x1 108 us: per_device(): half = lax.psum(inner_gram(residual, residual), 'vec')]
  transfers between devices with their start and end apart: 5 -> 7, of which waited for: 5 -> 6; matrix products, arithmetic and copies ran while one was open for 1% -> 2% of each run, Pallas kernels for 0% -> 0%
where the time goes in v1:
time: 1200 us; the launch traced here: 1190 us
  waiting for transfers between devices  694 us (58%)
  blocking collectives  211 us (18%)
  local copies, waits for them, and re-layouts  100 us (8%)
  other arithmetic  92.8 us (8%)
  matrix products  57.6 us (5%)
  starting transfers between devices  20.3 us (2%)
  between operations  16.2 us (1%)
    psum x2, waiting for transfers between devices, per_device(): curv_gram = lax.psum(inner_gram(direction, image_vec), ('arc', 'vec'))  273 us
    psum x1, waiting for transfers between devices, per_device(): new_gram = lax.psum(inner_gram(residual, residual), ('arc', 'vec'))  123 us
    psum x1, waiting for transfers between devices, per_device(): half = lax.psum(inner_gram(residual, residual), 'vec')  108 us
    all_to_all x1, blocking collectives, trade_back(): lax.all_to_all(buffer, ('arc', 'vec'), split_axis=0, concat_axis=0, tiled...  107 us
    all_to_all x1, waiting for transfers between devices, trade_out(): lax.all_to_all(buffer, ('arc', 'vec'), split_axis=0, concat_axis=0, tiled...  106 us
    all_to_all x1, blocking collectives, trade_out(): lax.all_to_all(buffer, ('arc', 'vec'), split_axis=0, concat_axis=0, tiled...  104 us
    psum x1, waiting for transfers between devices, per_device(): res_gram = lax.psum(half, 'arc')  83.4 us
    scatter x2, local copies, waits for them, and re-layouts, per_device(): returning = jnp.zeros((device_count * slot_count, block_rows, rhs_count),...  38.6 us
  transfers between devices with their start and end apart: 7, of which 6 were waited for; matrix products, arithmetic and copies ran while one was open for 2% of the time, Pallas kernels for 0%

profile of v1, /device:TPU:1, one launch (start us, length us, event | category | flops | bytes accessed | tf_op | source)
XLA Modules:
  0.0 1191.8 jit_solution(5083724130027614488)
XLA Ops:
  18.5 8.3 gather_fusion
  26.9 7.2 broadcast_select_fusion.1
  34.1 12.3 %all-to-all-start = ((bf16[256,128,128]{2,1,0:T(8,128)(2,1)}), bf16[256,128,128]{2,1,0:T(8,128)(2,1)}, u32[]{:S(2)}, u32[]{:S(2)}) async-start(bf16[256,128,128]{2,1,0:T(8,128)(2,1)} %broadcast_select_fusion.1), calls=%async_computation | async-start | bytes 16777216 | tf_op jit(solution)/shard_map/all_to_all | solution.py:18
  46.5 106.4 %all-to-all-done = bf16[256,128,128]{2,1,0:T(8,128)(2,1)} async-done(((bf16[256,128,128]{2,1,0:T(8,128)(2,1)}), bf16[256,128,128]{2,1,0:T(8,128)(2,1)}, u32[]{:S(2)}, u32[]{:S(2)}) %all-to-all-start) | async-done | bytes 8388640 | tf_op jit(solution)/shard_map/all_to_all | solution.py:18
  152.9 6.4 gather_fusion.1
  159.3 8.2 convolution_convert_fusion.4
  167.5 6.9 convert_bitcast_fusion.1
  174.5 6.4 copy.140
  186.2 19.3 %scatter_fusion = bf16[256,128,128]{2,1,0:T(8,128)(2,1)} fusion(bf16[256,128,128]{2,1,0:T(8,128)(2,1)} %broadcast.116.clone, s32[128]{0:T(128)S(1)} %fusion.34, bf16[128,128,128]{2,1,0:T(8,128)(2,1)} %bitcast.106), kind=kCustom, calls=%fused_computation.4 | custom fusion | bytes 12583424 | tf_op jit(solution)/shard_map/scatter | solution.py:83
  205.5 6.8 all-to-all-start.1
  213.8 108.0 %all-reduce.8.cloned.1.call-done = f32[128,128]{0,1:T(8,128)} async-done(((f32[128,128]{0,1:T(8,128)}), f32[128,128]{0,1:T(8,128)}) %all-reduce.8.cloned.1.call-update) | async-done | bytes 65552 | tf_op jit(solution)/shard_map/psum | solution.py:58
  322.2 83.4 %all-reduce.10.cloned.1.call-done = f32[128,128]{0,1:T(8,128)} async-done(((f32[128,128]{0,1:T(8,128)}), f32[128,128]{0,1:T(8,128)}) %all-reduce.10.cloned.1.call-update) | async-done | bytes 65552 | tf_op jit(solution)/shard_map/psum | solution.py:59
  407.5 11.7 cholesky.70
  419.2 7.8 fusion.2
  429.5 137.4 %all-reduce.6.cloned.1.call-done = f32[128,128]{0,1:T(8,128)} async-done(((f32[128,128]{0,1:T(8,128)}), f32[128,128]{0,1:T(8,128)}) %all-reduce.6.cloned.1.call-update) | async-done | bytes 65552 | tf_op jit(solution)/shard_map/psum | solution.py:88
  568.7 11.7 cholesky.59
  581.7 9.8 custom-call.9
  595.9 9.8 custom-call.10
  605.7 122.7 %all-reduce.12.cloned.1.call-done = f32[128,128]{1,0:T(8,128)} async-done(((f32[128,128]{1,0:T(8,128)}), f32[128,128]{1,0:T(8,128)}) %all-reduce.12.cloned.1.call-update) | async-done | bytes 65552 | tf_op jit(solution)/shard_map/psum | solution.py:94
  730.3 8.3 gather_fusion.2
  738.6 7.2 broadcast_select_fusion
  745.9 103.9 %all_to_all.20 = bf16[256,128,128]{2,1,0:T(8,128)(2,1)} all-to-all(bf16[256,128,128]{2,1,0:T(8,128)(2,1)} %broadcast_select_fusion), channel_id=1, replica_groups=mesh['arc'=16,'vec'=8] {'arc','vec'}, dimensions={0} | all-to-all | bytes 16777216 | tf_op jit(solution)/shard_map/all_to_all | solution.py:18
  849.7 6.4 gather_fusion.3
  856.2 9.2 convolution_convert_fusion.1
  865.4 7.2 convert_bitcast_fusion
  872.6 6.4 copy.153
  879.0 5.3 broadcast.116
  884.3 19.4 %scatter_fusion.1 = bf16[256,128,128]{2,1,0:T(8,128)(2,1)} fusion(bf16[256,128,128]{2,1,0:T(8,128)(2,1)} %broadcast.116, s32[128]{0:T(128)S(1)} %fusion.34, bf16[128,128,128]{2,1,0:T(8,128)(2,1)} %bitcast.105), kind=kCustom, calls=%fused_computation.5 | custom fusion | bytes 12583424 | tf_op jit(solution)/shard_map/scatter | solution.py:83
  903.7 106.9 %all_to_all.21 = bf16[256,128,128]{2,1,0:T(8,128)(2,1)S(1)} all-to-all(bf16[256,128,128]{2,1,0:T(8,128)(2,1)} %scatter_fusion.1), channel_id=1, replica_groups=mesh['arc'=16,'vec'=8] {'arc','vec'}, dimensions={0} | all-to-all | bytes 16777216 | tf_op jit(solution)/shard_map/all_to_all | solution.py:22
  1018.5 135.7 %all-reduce.14.cloned.1.call-done = f32[128,128]{0,1:T(8,128)} async-done(((f32[128,128]{0,1:T(8,128)}), f32[128,128]{0,1:T(8,128)}) %all-reduce.14.cloned.1.call-update) | async-done | bytes 65552 | tf_op jit(solution)/shard_map/psum | solution.py:88
  1156.0 11.7 cholesky.81
  1169.0 9.8 custom-call.11
  (77 shorter events, 47.3 us)
Async XLA Ops:
  8.0 151.3 %copy-start = (bf16[16,256,256]{2,1,0:T(8,128)(2,1)S(1)}, bf16[16,256,256]{2,1,0:T(8,128)(2,1)}, u32[]{:S(2)}) copy-start(bf16[16,256,256]{2,1,0:T(8,128)(2,1)} %param.11) | copy-start | bytes 6291460
  34.1 118.8 %all-to-all-start = ((bf16[256,128,128]{2,1,0:T(8,128)(2,1)}), bf16[256,128,128]{2,1,0:T(8,128)(2,1)}, u32[]{:S(2)}, u32[]{:S(2)}) async-start(bf16[256,128,128]{2,1,0:T(8,128)(2,1)} %broadcast_select_fusion.1), calls=%async_computation | async-start | bytes 16777216 | tf_op jit(solution)/shard_map/all_to_all | solution.py:18
  205.5 6.9 copy-start.1
  205.5 213.7 %all-to-all-start.1 = ((bf16[256,128,128]{2,1,0:T(8,128)(2,1)}), bf16[256,128,128]{2,1,0:T(8,128)(2,1)}, u32[]{:S(2)}, u32[]{:S(2)}) async-start(bf16[256,128,128]{2,1,0:T(8,128)(2,1)} %scatter_fusion), calls=%async_computation.1 | async-start | bytes 16777216 | tf_op jit(solution)/shard_map/all_to_all | solution.py:22
  212.3 214.8 %copy-start.6 = (f32[5,128]{1,0:T(8,128)S(1)}, f32[5,128]{1,0:T(8,128)}, u32[]{:S(2)}) copy-start(f32[5,128]{1,0:T(8,128)} %param.10) | copy-start | bytes 7684
  212.3 109.5 %all-reduce.8.cloned.1.call-start = ((), (), s32[]{:S(2)}) async-start(), calls=%async_computation.5 | async-start | bytes 131072 | tf_op jit(solution)/shard_map/psum | solution.py:58
  213.7 191.9 %all-reduce.10.cloned.1.call-start = ((), (), s32[]{:S(2)}) async-start(), calls=%async_computation.6 | async-start | bytes 131072 | tf_op jit(solution)/shard_map/psum | solution.py:59
  321.8 245.1 %all-reduce.6.cloned.1.call-start = ((), (), s32[]{:S(2)}) async-start(), calls=%async_computation.4 | async-start | bytes 131072 | tf_op jit(solution)/shard_map/psum | solution.py:88
  405.6 186.0 %copy-start.3 = (f32[128,128]{0,1:T(8,128)S(1)}, f32[128,128]{0,1:T(8,128)}, u32[]{:S(2)}) copy-start(f32[128,128]{0,1:T(8,128)} %all-reduce.10.cloned.1.call-done) | copy-start | bytes 196612
  419.2 10.3 copy-start.5
  428.5 299.9 %all-reduce.12.cloned.1.call-start = ((), (), s32[]{:S(2)}) async-start(), calls=%async_computation.7 | async-start | bytes 131072 | tf_op jit(solution)/shard_map/psum | solution.py:94
  593.9 560.3 %all-reduce.14.cloned.1.call-start = ((), (), s32[]{:S(2)}) async-start(), calls=%async_computation.8 | async-start | bytes 131072 | tf_op jit(solution)/shard_map/psum | solution.py:88
  1010.6 168.3 %copy-start.4 = (f32[128,128]{1,0:T(8,128)S(1)}, f32[128,128]{1,0:T(8,128)}, u32[]{:S(2)}) copy-start(f32[128,128]{1,0:T(8,128)} %all-reduce.12.cloned.1.call-done) | copy-start | bytes 196612
  1015.0 0.8 copy-start.2
Sparse Core Ops, SparseCore 0:
  216.0 105.7 all-reduce.7
  325.3 80.2 all-reduce.9
Sparse Core Ops, SparseCore 1:
  428.6 138.2 all-reduce.5
  594.0 134.4 all-reduce.11
  1017.4 136.7 all-reduce.13
